TPU v7x, 256 devices: a whole 4x4x8 slice. The times are simulated.
256 devices in a mesh: row: 8 (over x, core), rhs: 32 (over y, z).
Axes of the slice: x: 4, y: 4, z: 8, core: 2. Of those that a mesh axis runs over, the one named last changes fastest.
Arguments:
- local_rhs: bfloat16 [336, 128, 4096], P('row', None, 'rhs'), may hold values from -6 to 6
- top_rhs: bfloat16 [8, 128, 4096], P('row', None, 'rhs'), may hold values from -6 to 6
- diag_inv: bfloat16 [336, 128, 128], P('row', 'rhs'), as said below
- top_inv: bfloat16 [8, 128, 128], P('row', 'rhs'), as said below
- off_blocks: bfloat16 [336, 4, 128, 128], P('row', None, 'rhs'), may hold values from -0.125 to 0.125
- top_factor: bfloat16 [8, 8, 128, 128], P('row', None, 'rhs'), may hold values from -0.1875 to 0.1875
- targets: int32 [336, 4], P('row'), may hold values from 24 to 49, as said below
Outputs:
- local_solution: bfloat16 [336, 128, 4096], P('row', None, 'rhs')
- top_solution: bfloat16 [8, 128, 4096], P('row', None, 'rhs')
Inputs may be any that keep to these rules, and one draw needn't show every extreme that they name: `diag_inv`: each block is lower triangular. `top_inv`: each block is lower triangular. `targets`: row r * 42 + k holds 4 distinct codes; a code c < 42 names local supernode r * 42 + c, of a higher level than k; a code c >= 42 names top block c - 42.
All inputs are finite; a program needn't handle non-finite values.
Results may differ from a plain program's by a relative error of at most 0.023.
Values may be sent and summed in bfloat16 or wider, within the bound.
No kernel may reach another device: no remote copies, remote signals or barrier semaphores. Data moves between devices by JAX's collectives and lax.ppermute only.
A program may use at most 64 MiB of HBM per device.

v0:
```python
import jax
import jax.numpy as jnp
from jax import lax
from jax.sharding import PartitionSpec as P

LEAF = 24


def spread(shard, axis, root):
    mine = lax.axis_index(axis) == root
    return lax.psum(jnp.where(mine, shard, jnp.zeros_like(shard)), axis)


def local(local_rhs, top_rhs, diag_inv, top_inv, off_blocks, top_factor, targets):
    sub_count = local_rhs.shape[0]
    panel_width = local_rhs.shape[1]
    columns = local_rhs.shape[2]
    top_count = lax.axis_size("row")
    cand_count = sub_count + top_count
    acc_local = jnp.zeros((sub_count, panel_width, columns), jnp.float32)
    acc_top = jnp.zeros((top_count, panel_width, columns), jnp.float32)
    level_ranges = ((0, LEAF), (LEAF, LEAF + LEAF // 2), (LEAF + LEAF // 2, sub_count))
    solved = []
    for first_row, end_row in level_ranges:
        residual_rows = (
            local_rhs[first_row:end_row].astype(jnp.float32) - acc_local[first_row:end_row]
        ).astype(jnp.bfloat16)

        def apply_inverse(slice_part, offset, residual_rows=residual_rows):
            return jnp.einsum(
                "jxm,jme->jxe", slice_part, residual_rows, preferred_element_type=jnp.float32
            )

        level_partial = apply_inverse(
            lax.all_gather(diag_inv[first_row:end_row], "rhs", axis=1, tiled=True), jnp.int32(0)
        ).astype(jnp.bfloat16)
        solved.append(level_partial)
        target_codes = targets[first_row:end_row].reshape(-1)
        later_count = cand_count - end_row
        selector = (
            jnp.arange(later_count, dtype=jnp.int32)[:, None] == target_codes[None, :] - end_row
        ).astype(jnp.float32)

        def spread_updates(slice_part, offset, level_partial=level_partial, selector=selector):
            products = jnp.einsum(
                "yiko,yoq->yikq", slice_part, level_partial, preferred_element_type=jnp.float32
            )
            flattened = products.reshape(selector.shape[1], slice_part.shape[2], columns)
            return jnp.einsum("cn,nar->car", selector, flattened, precision=lax.Precision.HIGHEST)

        contrib = spread_updates(
            lax.all_gather(off_blocks[first_row:end_row], "rhs", axis=2, tiled=True), jnp.int32(0)
        )
        acc_local = acc_local.at[end_row:].add(contrib[: sub_count - end_row])
        acc_top = acc_top + contrib[sub_count - end_row :]
    inverse_rows = top_inv.reshape(1, 1, top_inv.shape[1], panel_width)
    top_full, inv_full = (
        lax.all_gather(top_factor, "rhs", axis=2, tiled=True),
        lax.all_gather(inverse_rows, "rhs", axis=2, tiled=True),
    )
    position = lax.axis_index("row")
    own_sum = lax.psum_scatter(
        acc_top.astype(jnp.bfloat16), "row", scatter_dimension=0, tiled=True
    ).astype(jnp.float32)
    base_value = top_rhs[0].astype(jnp.float32) - own_sum[0]

    def top_step(step_index, carry):
        carried, own_solution = carry
        residual_rows = (base_value - carried).astype(jnp.bfloat16)
        candidate = jnp.dot(
            inv_full[0, 0], residual_rows, preferred_element_type=jnp.float32
        ).astype(jnp.bfloat16)
        solution = spread(candidate, "row", step_index)
        own_solution = jnp.where(position == step_index, solution, own_solution)
        coupling_matrix = lax.dynamic_index_in_dim(top_full[0], step_index, 0, keepdims=False)
        update = jnp.dot(coupling_matrix, solution, preferred_element_type=jnp.float32)
        carried = carried + jnp.where(step_index < position, update, 0.0)
        return (carried, own_solution)

    initial_state = (
        jnp.zeros((panel_width, columns), jnp.float32),
        jnp.zeros((panel_width, columns), jnp.bfloat16),
    )
    own_separator = lax.fori_loop(0, top_count, top_step, initial_state)[1][None]
    return (jnp.concatenate(solved, axis=0), own_separator)


def solution(mesh):
    in_specs = (
        P("row", None, "rhs"),
        P("row", None, "rhs"),
        P("row", "rhs", None),
        P("row", "rhs", None),
        P("row", None, "rhs", None),
        P("row", None, "rhs", None),
        P("row", None),
    )
    out_specs = (P("row", None, "rhs"), P("row", None, "rhs"))
    return jax.shard_map(local, mesh=mesh, in_specs=in_specs, out_specs=out_specs, check_vma=False)
```

profile of v0, /device:TPU:16, one launch (start us, length us, event | category | flops | bytes accessed | tf_op | source)
XLA Modules:
  0.0 551.3 jit_solution(5138594552302585885)
XLA Ops:
  7.3 0.9 slice.103
  8.2 0.7 copy.121
  8.9 0.9 slice.109
  9.9 0.6 copy.124
  10.6 0.8 slice.99
  12.1 54.8 %all_gather.28 = bf16[6,128,128]{2,0,1:T(8,128)(2,1)} all-gather(bf16[6,4,128]{2,0,1:T(8,128)(2,1)S(1)} %copy.125), channel_id=1, replica_groups=mesh['row'=8,'rhs'=32] {'rhs'}, dimensions={1}, use_global_device_ids=true | all-gather | bytes 202752 | tf_op jit(solution)/shard_map/all_gather | solution.py:35
  66.9 48.5 %all_gather.26 = bf16[12,128,128]{2,0,1:T(8,128)(2,1)S(1)} all-gather(bf16[12,4,128]{2,0,1:T(8,128)(2,1)S(1)} %copy.122), channel_id=1, replica_groups=mesh['row'=8,'rhs'=32] {'rhs'}, dimensions={1}, use_global_device_ids=true | all-gather | bytes 405504 | tf_op jit(solution)/shard_map/all_gather | solution.py:35
  115.4 47.8 %all_gather.24 = bf16[24,128,128]{2,0,1:T(8,128)(2,1)S(1)} all-gather(bf16[24,4,128]{2,0,1:T(8,128)(2,1)S(1)} %copy.119), channel_id=1, replica_groups=mesh['row'=8,'rhs'=32] {'rhs'}, dimensions={1}, use_global_device_ids=true | all-gather | bytes 811008 | tf_op jit(solution)/shard_map/all_gather | solution.py:35
  163.2 53.6 %all_gather.30 = bf16[6,4,128,128]{3,1,0,2:T(4,128)(2,1)} all-gather(bf16[6,4,4,128]{3,1,0,2:T(4,128)(2,1)S(1)} %copy.126), channel_id=1, replica_groups=mesh['row'=8,'rhs'=32] {'rhs'}, dimensions={2}, use_global_device_ids=true | all-gather | bytes 811008 | tf_op jit(solution)/shard_map/all_gather | solution.py:52
  216.9 0.4 convolution_convert_fusion.1
  217.3 7.2 %fusion.10 = f32[24,128,4,128]{3,1,2,0:T(8,128)} fusion(bf16[24,4,128,128]{3,0,1,2:T(8,128)(2,1)} %all-gather.4.cloned.1.call-done, bf16[24,128,128]{2,1,0:T(8,128)(2,1)S(1)} %convolution_convert_fusion.1), kind=kOutput, calls=%fused_computation.14 | convolution fusion | flops 402653184 | bytes 10223616 | tf_op jit(solution)/shard_map/yiko,yoq->yikq/dot_general | solution.py:45
  224.5 6.7 %copy.82 = f32[96,128,128]{2,0,1:T(8,128)} copy(f32[96,128,128]{1,2,0:T(8,128)} %bitcast.61) | data formatting | bytes 12582912 | tf_op jit(solution)/shard_map/reshape | solution.py:48
  231.2 4.5 fusion.30
  235.8 1.4 copy-done
  237.1 0.3 fusion.15
  237.4 0.3 convolution_convert_fusion.2
  237.8 3.8 fusion.12
  241.6 2.6 copy.92
  244.2 1.2 fusion.34
  245.4 1.9 fusion.22
  247.3 0.2 convolution_convert_fusion.3
  247.5 1.6 fusion.17
  249.1 2.0 copy.102
  251.2 2.0 fusion.14
  253.2 0.8 copy.103
  254.0 46.4 %all_gather.29 = bf16[1,8,128,128]{3,1,0,2:T(8,128)(2,1)S(1)} all-gather(bf16[1,8,4,128]{3,1,0,2:T(8,128)(2,1)S(1)} %copy.97), channel_id=1, replica_groups=mesh['row'=8,'rhs'=32] {'rhs'}, dimensions={2}, use_global_device_ids=true | all-gather | bytes 270336 | tf_op jit(solution)/shard_map/all_gather | solution.py:58
  300.5 48.1 %all-gather = bf16[1,128,128]{2,0,1:T(2,128)(2,1)S(1)} all-gather(bf16[1,4,128]{2,0,1:T(2,128)(2,1)S(1)} %copy.104), channel_id=2, replica_groups=mesh['row'=8,'rhs'=32] {'rhs'}, dimensions={1}, use_global_device_ids=true | all-gather | bytes 33792 | tf_op jit(solution)/shard_map/all_gather | solution.py:59
  348.7 2.3 pad_maximum_fusion
  351.0 0.8 subtract_bitcast_fusion
  351.8 192.2 %while.18 = (s32[]{:T(128)}, f32[128,128]{1,0:T(8,128)S(1)}, bf16[128,128]{0,1:T(8,128)(2,1)S(1)}, s32[]{:T(128)}, bf16[1,8,128,128]{3,2,1,0:T(8,128)(2,1)S(1)},...) while((s32[]{:T(128)}, f32[128,128]{1,0:T(8,128)S(1)}, ...), condition=%wide.region_3.4_spmd.clone, body=%wide.region_1.3_spmd.clone.sunk | while | flops 8568841 | bytes 557243 | solution.py:84
  351.8 0.2 fusion.52
  352.0 23.6 %psum.13 = bf16[128,128]{0,1:T(8,128)(2,1)S(1)} all-reduce(bf16[128,128]{0,1:T(8,128)(2,1)S(1)} %fusion.52), channel_id=1, replica_groups=mesh['row'=8,'rhs'=32] {'row'}, use_global_device_ids=true, to_apply=%region_2.2 | all-reduce | flops 16384 | bytes 65536 | tf_op jit(solution)/shard_map/while/body/eval_jaxpr/psum | solution.py:11
  375.6 0.2 fusion.53
  375.9 0.2 fusion.52
  376.1 23.6 %psum.13 = bf16[128,128]{0,1:T(8,128)(2,1)S(1)} all-reduce(bf16[128,128]{0,1:T(8,128)(2,1)S(1)} %fusion.52), channel_id=1, replica_groups=mesh['row'=8,'rhs'=32] {'row'}, use_global_device_ids=true, to_apply=%region_2.2 | all-reduce | flops 16384 | bytes 65536 | tf_op jit(solution)/shard_map/while/body/eval_jaxpr/psum | solution.py:11
  399.9 0.2 fusion.52
  400.1 23.6 %psum.13 = bf16[128,128]{0,1:T(8,128)(2,1)S(1)} all-reduce(bf16[128,128]{0,1:T(8,128)(2,1)S(1)} %fusion.52), channel_id=1, replica_groups=mesh['row'=8,'rhs'=32] {'row'}, use_global_device_ids=true, to_apply=%region_2.2 | all-reduce | flops 16384 | bytes 65536 | tf_op jit(solution)/shard_map/while/body/eval_jaxpr/psum | solution.py:11
  423.9 0.2 fusion.52
  424.1 23.6 %psum.13 = bf16[128,128]{0,1:T(8,128)(2,1)S(1)} all-reduce(bf16[128,128]{0,1:T(8,128)(2,1)S(1)} %fusion.52), channel_id=1, replica_groups=mesh['row'=8,'rhs'=32] {'row'}, use_global_device_ids=true, to_apply=%region_2.2 | all-reduce | flops 16384 | bytes 65536 | tf_op jit(solution)/shard_map/while/body/eval_jaxpr/psum | solution.py:11
  447.9 0.2 fusion.52
  448.1 23.6 %psum.13 = bf16[128,128]{0,1:T(8,128)(2,1)S(1)} all-reduce(bf16[128,128]{0,1:T(8,128)(2,1)S(1)} %fusion.52), channel_id=1, replica_groups=mesh['row'=8,'rhs'=32] {'row'}, use_global_device_ids=true, to_apply=%region_2.2 | all-reduce | flops 16384 | bytes 65536 | tf_op jit(solution)/shard_map/while/body/eval_jaxpr/psum | solution.py:11
  471.9 0.2 fusion.52
  472.1 23.6 %psum.13 = bf16[128,128]{0,1:T(8,128)(2,1)S(1)} all-reduce(bf16[128,128]{0,1:T(8,128)(2,1)S(1)} %fusion.52), channel_id=1, replica_groups=mesh['row'=8,'rhs'=32] {'row'}, use_global_device_ids=true, to_apply=%region_2.2 | all-reduce | flops 16384 | bytes 65536 | tf_op jit(solution)/shard_map/while/body/eval_jaxpr/psum | solution.py:11
  496.0 0.2 fusion.52
  496.2 23.6 %psum.13 = bf16[128,128]{0,1:T(8,128)(2,1)S(1)} all-reduce(bf16[128,128]{0,1:T(8,128)(2,1)S(1)} %fusion.52), channel_id=1, replica_groups=mesh['row'=8,'rhs'=32] {'row'}, use_global_device_ids=true, to_apply=%region_2.2 | all-reduce | flops 16384 | bytes 65536 | tf_op jit(solution)/shard_map/while/body/eval_jaxpr/psum | solution.py:11
  520.0 0.2 fusion.52
  520.2 23.6 %psum.13 = bf16[128,128]{0,1:T(8,128)(2,1)S(1)} all-reduce(bf16[128,128]{0,1:T(8,128)(2,1)S(1)} %fusion.52), channel_id=1, replica_groups=mesh['row'=8,'rhs'=32] {'row'}, use_global_device_ids=true, to_apply=%region_2.2 | all-reduce | flops 16384 | bytes 65536 | tf_op jit(solution)/shard_map/while/body/eval_jaxpr/psum | solution.py:11
  544.0 0.7 copy.106
  (80 shorter events, 2.3 us)
Async XLA Ops:
  7.2 4.7 slice-start.2
  7.2 4.4 slice-start.3
  7.2 4.6 slice-start.4
  7.2 4.1 copy-start.11
  7.2 210.0 %all-gather.4.cloned.1.call-start = ((), (), s32[]{:S(2)}) async-start(), calls=%async_computation.1 | async-start | bytes 3244032 | tf_op jit(solution)/shard_map/all_gather | solution.py:52
  8.9 208.0 %copy-start.8 = (bf16[42,128,128]{2,1,0:T(8,128)(2,1)S(1)}, bf16[42,128,128]{2,1,0:T(8,128)(2,1)}, u32[]{:S(2)}) copy-start(bf16[42,128,128]{2,1,0:T(8,128)(2,1)} %param.13) | copy-start | bytes 4128772
  8.9 228.9 %all-gather.6.cloned.1.call-start = ((), (), s32[]{:S(2)}) async-start(), calls=%async_computation.2 | async-start | bytes 1622016 | tf_op jit(solution)/shard_map/all_gather | solution.py:52
  10.5 340.5 %reduce-scatter.2.cloned.1.call-start = ((), (), s32[]{:S(2)}) async-start(), calls=%async_computation.3 | async-start | bytes 294912 | tf_op jit(solution)/shard_map/reduce_scatter | solution.py:62
  217.2 7.3 %copy-start.1 = (bf16[24,128,128]{2,1,0:T(8,128)(2,1)}, bf16[24,128,128]{2,1,0:T(8,128)(2,1)S(1)}, u32[]{:S(2)}) copy-start(bf16[24,128,128]{2,1,0:T(8,128)(2,1)S(1)} %convolution_convert_fusion.1) | copy-start | bytes 2359300
  231.2 5.9 %slice-start = ((bf16[42,128,128]{2,1,0:T(8,128)(2,1)}), bf16[12,128,128]{2,1,0:T(8,128)(2,1)S(1)}, s32[]{:S(2)}) async-start(bf16[42,128,128]{2,1,0:T(8,128)(2,1)} %param.13), calls=%async_computation.4 | async-start | bytes 786432 | tf_op jit(solution)/shard_map/slice | solution.py:26
  235.7 1.4 copy-start
  237.7 3.8 copy-start.5
  244.1 1.2 slice-start.1
  244.2 3.1 copy-start.9
  245.4 3.7 copy-start.3
  245.4 2.1 copy-start.6
  247.5 1.6 copy-start.7
  249.1 2.1 copy-start.4
  251.2 2.9 copy-start.12
  251.2 49.3 %copy-start.13 = (bf16[1,4,128]{2,1,0:T(4,128)(2,1)S(1)}, bf16[1,4,128]{2,1,0:T(4,128)(2,1)}, u32[]{:S(2)}) copy-start(bf16[1,4,128]{2,1,0:T(4,128)(2,1)} %param.16) | copy-start | bytes 3076
  251.2 97.5 %copy-start.2 = (bf16[24,128,128]{2,1,0:T(8,128)(2,1)S(1)}, bf16[24,128,128]{2,1,0:T(8,128)(2,1)}, u32[]{:S(2)}) copy-start(bf16[24,128,128]{2,1,0:T(8,128)(2,1)} %copy-done.1) | copy-start | bytes 2359300
  254.0 97.1 %copy-start.10 = (bf16[1,128,128]{2,1,0:T(8,128)(2,1)S(1)}, bf16[1,128,128]{2,1,0:T(8,128)(2,1)}, u32[]{:S(2)}) copy-start(bf16[1,128,128]{2,1,0:T(8,128)(2,1)} %param.14) | copy-start | bytes 98308
Sparse Core Ops, SparseCore 0:
  11.2 81.3 all-gather.3
  95.1 74.5 all-gather.5
  254.1 30.7 reduce-scatter.1
where the time goes:
time: 552 us; the launch traced here: 551 us
  blocking collectives  488 us (88%)
  matrix products  23.9 us (4%)
  local copies, waits for them, and re-layouts  18.8 us (3%)
  between operations  14.2 us (3%)
  other arithmetic  5.59 us (1%)
    psum x8, blocking collectives, spread(): return lax.psum(jnp.where(mine, shard, jnp.zeros_like(shard)), axis)  189 us
    all_gather x3, blocking collectives, local(): lax.all_gather(diag_inv[first_row:end_row], 'rhs', axis=1, tiled=True)  151 us
    all_gather x1, blocking collectives, local(): lax.all_gather(off_blocks[first_row:end_row], 'rhs', axis=2, tiled=True)  53.6 us
    all_gather x1, blocking collectives, local(): lax.all_gather(inverse_rows, 'rhs', axis=2, tiled=True)  48.1 us
    all_gather x1, blocking collectives, local(): lax.all_gather(top_factor, 'rhs', axis=2, tiled=True)  46.4 us
    dot_general x3, matrix products, spread_updates(): jnp.einsum('yiko,yoq->yikq', slice_part, level_partial, preferred_element...  12.6 us
    reshape x3, local copies, waits for them, and re-layouts, spread_updates(): products.reshape(selector.shape[1], slice_part.shape[2], columns)  11.4 us
  transfers between devices with their start and end apart: 3, of which 0 were waited for; matrix products, arithmetic and copies ran while one was open for 5% of the time, Pallas kernels for 0%

commit v1 on v0

--- a/solution.py
+++ b/solution.py
@@ -55,7 +55,9 @@
         acc_top = acc_top + contrib[sub_count - end_row :]
     inverse_rows = top_inv.reshape(1, 1, top_inv.shape[1], panel_width)
     top_full, inv_full = (
-        lax.all_gather(top_factor, "rhs", axis=2, tiled=True),
+        jnp.concatenate(
+            lax.all_to_all(jnp.stack([top_factor] * lax.axis_size("rhs")), "rhs", 0, 0), axis=2
+        ),
         lax.all_gather(inverse_rows, "rhs", axis=2, tiled=True),
     )
     position = lax.axis_index("row")

time: 552 us -> 516 us (0.935)
  blocking collectives: 488 us -> 437 us
  starting transfers between devices: 0.12 us -> 11.8 us
    all_gather x1 -> x0, blocking collectives: 46.4 us -> none  [local(): lax.all_gather(top_factor, 'rhs', axis=2, tiled=True)]
    all_to_all x0 -> x1, starting transfers between devices: none -> 11.6 us  [local(): lax.all_to_all(jnp.stack([top_factor] * lax.axis_size('rhs')), 'rhs', 0, 0)]
  transfers between devices with their start and end apart: 3 -> 4, of which waited for: 0 -> 0; matrix products, arithmetic and copies ran while one was open for 5% -> 8% of each run, Pallas kernels for 0% -> 0%
where the time goes in v1:
time: 516 us; the launch traced here: 514 us
  blocking collectives  437 us (85%)
  matrix products  23.9 us (5%)
  local copies, waits for them, and re-layouts  20.4 us (4%)
  between operations  14.2 us (3%)
  starting transfers between devices  11.8 us (2%)
  other arithmetic  5.59 us (1%)
    psum x8, blocking collectives, spread(): return lax.psum(jnp.where(mine, shard, jnp.zeros_like(shard)), axis)  189 us
    all_gather x3, blocking collectives, local(): lax.all_gather(diag_inv[first_row:end_row], 'rhs', axis=1, tiled=True)  149 us
    all_gather x1, blocking collectives, local(): lax.all_gather(off_blocks[first_row:end_row], 'rhs', axis=2, tiled=True)  52.6 us
    all_gather x1, blocking collectives, local(): lax.all_gather(inverse_rows, 'rhs', axis=2, tiled=True)  46.8 us
    dot_general x3, matrix products, spread_updates(): jnp.einsum('yiko,yoq->yikq', slice_part, level_partial, preferred_element...  12.6 us
    all_to_all x1, starting transfers between devices, local(): lax.all_to_all(jnp.stack([top_factor] * lax.axis_size('rhs')), 'rhs', 0, 0)  11.6 us
    reshape x3, local copies, waits for them, and re-layouts, spread_updates(): products.reshape(selector.shape[1], slice_part.shape[2], columns)  11.4 us
  transfers between devices with their start and end apart: 4, of which 0 were waited for; matrix products, arithmetic and copies ran while one was open for 8% of the time, Pallas kernels for 0%

profile of v1, /device:TPU:16, one launch (start us, length us, event | category | flops | bytes accessed | tf_op | source)
XLA Modules:
  0.0 513.7 jit_solution(3233924086404575733)
XLA Ops:
  7.3 0.9 slice.103
  8.2 0.7 copy.119
  8.9 0.8 slice.109
  9.8 0.6 copy.122
  10.4 1.5 stack.2
  11.9 11.6 %all-to-all-start = ((bf16[32,1,8,4,128]{4,3,2,1,0:T(4,128)(2,1)}), bf16[32,1,8,4,128]{4,3,2,1,0:T(4,128)(2,1)}, u32[]{:S(2)}, u32[]{:S(2)}) async-start(bf16[32,1,8,4,128]{4,3,2,1,0:T(4,128)(2,1)} %stack.2), calls=%async_computation | async-start | bytes 524288 | tf_op jit(solution)/shard_map/all_to_all | solution.py:59
  24.4 52.9 %all_gather.25 = bf16[6,128,128]{2,0,1:T(8,128)(2,1)} all-gather(bf16[6,4,128]{2,0,1:T(8,128)(2,1)S(1)} %copy.123), channel_id=1, replica_groups=mesh['row'=8,'rhs'=32] {'rhs'}, dimensions={1}, use_global_device_ids=true | all-gather | bytes 202752 | tf_op jit(solution)/shard_map/all_gather | solution.py:35
  77.3 47.7 %all_gather.23 = bf16[12,128,128]{2,0,1:T(8,128)(2,1)S(1)} all-gather(bf16[12,4,128]{2,0,1:T(8,128)(2,1)S(1)} %copy.120), channel_id=1, replica_groups=mesh['row'=8,'rhs'=32] {'rhs'}, dimensions={1}, use_global_device_ids=true | all-gather | bytes 405504 | tf_op jit(solution)/shard_map/all_gather | solution.py:35
  125.0 48.5 %all_gather.21 = bf16[24,128,128]{2,0,1:T(8,128)(2,1)S(1)} all-gather(bf16[24,4,128]{2,0,1:T(8,128)(2,1)S(1)} %copy.117), channel_id=1, replica_groups=mesh['row'=8,'rhs'=32] {'rhs'}, dimensions={1}, use_global_device_ids=true | all-gather | bytes 811008 | tf_op jit(solution)/shard_map/all_gather | solution.py:35
  173.5 52.6 %all_gather.26 = bf16[6,4,128,128]{3,1,0,2:T(4,128)(2,1)} all-gather(bf16[6,4,4,128]{3,1,0,2:T(4,128)(2,1)S(1)} %copy.124), channel_id=1, replica_groups=mesh['row'=8,'rhs'=32] {'rhs'}, dimensions={2}, use_global_device_ids=true | all-gather | bytes 811008 | tf_op jit(solution)/shard_map/all_gather | solution.py:52
  226.1 0.4 convolution_convert_fusion.1
  226.5 7.2 %fusion.10 = f32[24,128,4,128]{3,1,2,0:T(8,128)} fusion(bf16[24,4,128,128]{3,0,1,2:T(8,128)(2,1)} %all-gather.4.cloned.1.call-done, bf16[24,128,128]{2,1,0:T(8,128)(2,1)S(1)} %convolution_convert_fusion.1), kind=kOutput, calls=%fused_computation.14 | convolution fusion | flops 402653184 | bytes 10223616 | tf_op jit(solution)/shard_map/yiko,yoq->yikq/dot_general | solution.py:45
  233.7 6.7 %copy.81 = f32[96,128,128]{2,0,1:T(8,128)} copy(f32[96,128,128]{1,2,0:T(8,128)} %bitcast.66) | data formatting | bytes 12582912 | tf_op jit(solution)/shard_map/reshape | solution.py:48
  240.4 4.5 fusion.30
  245.0 1.3 copy-done
  246.3 0.3 fusion.15
  246.7 0.3 convolution_convert_fusion.2
  247.0 3.8 fusion.12
  250.8 2.6 copy.91
  253.4 1.2 fusion.34
  254.6 1.9 fusion.22
  256.5 0.2 convolution_convert_fusion.3
  256.7 1.6 fusion.17
  258.3 2.0 copy.100
  260.4 2.0 fusion.14
  262.4 0.7 copy.101
  263.2 46.8 %all-gather = bf16[1,128,128]{2,0,1:T(2,128)(2,1)S(1)} all-gather(bf16[1,4,128]{2,0,1:T(2,128)(2,1)S(1)} %copy.102), channel_id=2, replica_groups=mesh['row'=8,'rhs'=32] {'rhs'}, dimensions={1}, use_global_device_ids=true | all-gather | bytes 33792 | tf_op jit(solution)/shard_map/all_gather | solution.py:61
  310.1 1.0 copy.103
  311.1 2.3 pad_maximum_fusion
  313.5 0.8 subtract_bitcast_fusion
  314.2 192.2 %while.18 = (s32[]{:T(128)}, f32[128,128]{1,0:T(8,128)S(1)}, bf16[128,128]{0,1:T(8,128)(2,1)S(1)}, s32[]{:T(128)}, bf16[1,8,32,4,128]{4,3,2,1,0:T(4,128)(2,1)S(1...) while((s32[]{:T(128)}, f32[128,128]{1,0:T(8,128)S(1)}, ...), condition=%wide.region_3.4_spmd.clone, body=%wide.region_1.3_spmd.clone.sunk | while | flops 8568841 | bytes 557243 | solution.py:86
  314.3 0.2 fusion.52
  314.5 23.6 %psum.13 = bf16[128,128]{0,1:T(8,128)(2,1)S(1)} all-reduce(bf16[128,128]{0,1:T(8,128)(2,1)S(1)} %fusion.52), channel_id=1, replica_groups=mesh['row'=8,'rhs'=32] {'row'}, use_global_device_ids=true, to_apply=%region_2.2 | all-reduce | flops 16384 | bytes 65536 | tf_op jit(solution)/shard_map/while/body/eval_jaxpr/psum | solution.py:11
  338.3 0.2 fusion.52
  338.5 23.6 %psum.13 = bf16[128,128]{0,1:T(8,128)(2,1)S(1)} all-reduce(bf16[128,128]{0,1:T(8,128)(2,1)S(1)} %fusion.52), channel_id=1, replica_groups=mesh['row'=8,'rhs'=32] {'row'}, use_global_device_ids=true, to_apply=%region_2.2 | all-reduce | flops 16384 | bytes 65536 | tf_op jit(solution)/shard_map/while/body/eval_jaxpr/psum | solution.py:11
  362.3 0.2 fusion.52
  362.5 23.6 %psum.13 = bf16[128,128]{0,1:T(8,128)(2,1)S(1)} all-reduce(bf16[128,128]{0,1:T(8,128)(2,1)S(1)} %fusion.52), channel_id=1, replica_groups=mesh['row'=8,'rhs'=32] {'row'}, use_global_device_ids=true, to_apply=%region_2.2 | all-reduce | flops 16384 | bytes 65536 | tf_op jit(solution)/shard_map/while/body/eval_jaxpr/psum | solution.py:11
  386.3 0.2 fusion.52
  386.5 23.6 %psum.13 = bf16[128,128]{0,1:T(8,128)(2,1)S(1)} all-reduce(bf16[128,128]{0,1:T(8,128)(2,1)S(1)} %fusion.52), channel_id=1, replica_groups=mesh['row'=8,'rhs'=32] {'row'}, use_global_device_ids=true, to_apply=%region_2.2 | all-reduce | flops 16384 | bytes 65536 | tf_op jit(solution)/shard_map/while/body/eval_jaxpr/psum | solution.py:11
  410.4 0.2 fusion.52
  410.6 23.6 %psum.13 = bf16[128,128]{0,1:T(8,128)(2,1)S(1)} all-reduce(bf16[128,128]{0,1:T(8,128)(2,1)S(1)} %fusion.52), channel_id=1, replica_groups=mesh['row'=8,'rhs'=32] {'row'}, use_global_device_ids=true, to_apply=%region_2.2 | all-reduce | flops 16384 | bytes 65536 | tf_op jit(solution)/shard_map/while/body/eval_jaxpr/psum | solution.py:11
  434.4 0.2 fusion.52
  434.6 23.6 %psum.13 = bf16[128,128]{0,1:T(8,128)(2,1)S(1)} all-reduce(bf16[128,128]{0,1:T(8,128)(2,1)S(1)} %fusion.52), channel_id=1, replica_groups=mesh['row'=8,'rhs'=32] {'row'}, use_global_device_ids=true, to_apply=%region_2.2 | all-reduce | flops 16384 | bytes 65536 | tf_op jit(solution)/shard_map/while/body/eval_jaxpr/psum | solution.py:11
  458.4 0.2 fusion.52
  458.6 23.6 %psum.13 = bf16[128,128]{0,1:T(8,128)(2,1)S(1)} all-reduce(bf16[128,128]{0,1:T(8,128)(2,1)S(1)} %fusion.52), channel_id=1, replica_groups=mesh['row'=8,'rhs'=32] {'row'}, use_global_device_ids=true, to_apply=%region_2.2 | all-reduce | flops 16384 | bytes 65536 | tf_op jit(solution)/shard_map/while/body/eval_jaxpr/psum | solution.py:11
  482.4 0.2 fusion.52
  482.6 23.6 %psum.13 = bf16[128,128]{0,1:T(8,128)(2,1)S(1)} all-reduce(bf16[128,128]{0,1:T(8,128)(2,1)S(1)} %fusion.52), channel_id=1, replica_groups=mesh['row'=8,'rhs'=32] {'row'}, use_global_device_ids=true, to_apply=%region_2.2 | all-reduce | flops 16384 | bytes 65536 | tf_op jit(solution)/shard_map/while/body/eval_jaxpr/psum | solution.py:11
  506.4 0.7 copy.104
  (80 shorter events, 2.4 us)
Async XLA Ops:
  7.2 17.0 %slice-start.2 = ((bf16[42,4,4,128]{3,2,1,0:T(4,128)(2,1)}), bf16[6,4,4,128]{3,2,1,0:T(4,128)(2,1)S(1)}, s32[]{:S(2)}) async-start(bf16[42,4,4,128]{3,2,1,0:T(4,128)(2,1)} %param.17), calls=%async_computation.7 | async-start | bytes 49152 | tf_op jit(solution)/shard_map/slice | solution.py:52
  7.2 16.4 %slice-start.3 = ((bf16[42,4,128]{2,1,0:T(4,128)(2,1)}), bf16[24,4,128]{2,1,0:T(4,128)(2,1)S(1)}, s32[]{:S(2)}) async-start(bf16[42,4,128]{2,1,0:T(4,128)(2,1)} %param.15), calls=%async_computation.8 | async-start | bytes 49152 | tf_op jit(solution)/shard_map/slice | solution.py:35
  7.2 16.7 %slice-start.4 = ((bf16[42,4,128]{2,1,0:T(4,128)(2,1)}), bf16[12,4,128]{2,1,0:T(4,128)(2,1)S(1)}, s32[]{:S(2)}) async-start(bf16[42,4,128]{2,1,0:T(4,128)(2,1)} %param.15), calls=%async_computation.9 | async-start | bytes 24576 | tf_op jit(solution)/shard_map/slice | solution.py:35
  7.2 16.9 %slice-start.5 = ((bf16[42,4,128]{2,1,0:T(4,128)(2,1)}), bf16[6,4,128]{2,1,0:T(4,128)(2,1)S(1)}, s32[]{:S(2)}) async-start(bf16[42,4,128]{2,1,0:T(4,128)(2,1)} %param.15), calls=%async_computation.10 | async-start | bytes 12288 | tf_op jit(solution)/shard_map/slice | solution.py:35
  7.2 16.4 %copy-start.11 = (s32[42,4]{0,1:T(4,128)S(1)}, s32[42,4]{0,1:T(4,128)}, u32[]{:S(2)}) copy-start(s32[42,4]{0,1:T(4,128)} %param.19) | copy-start | bytes 2020
  7.2 219.3 %all-gather.4.cloned.1.call-start = ((), (), s32[]{:S(2)}) async-start(), calls=%async_computation.2 | async-start | bytes 3244032 | tf_op jit(solution)/shard_map/all_gather | solution.py:52
  8.9 238.1 %all-gather.6.cloned.1.call-start = ((), (), s32[]{:S(2)}) async-start(), calls=%async_computation.3 | async-start | bytes 1622016 | tf_op jit(solution)/shard_map/all_gather | solution.py:52
  11.9 298.2 %all-to-all-start = ((bf16[32,1,8,4,128]{4,3,2,1,0:T(4,128)(2,1)}), bf16[32,1,8,4,128]{4,3,2,1,0:T(4,128)(2,1)}, u32[]{:S(2)}, u32[]{:S(2)}) async-start(bf16[32,1,8,4,128]{4,3,2,1,0:T(4,128)(2,1)} %stack.2), calls=%async_computation | async-start | bytes 524288 | tf_op jit(solution)/shard_map/all_to_all | solution.py:59
  23.6 202.5 %copy-start.8 = (bf16[42,128,128]{2,1,0:T(8,128)(2,1)S(1)}, bf16[42,128,128]{2,1,0:T(8,128)(2,1)}, u32[]{:S(2)}) copy-start(bf16[42,128,128]{2,1,0:T(8,128)(2,1)} %param.13) | copy-start | bytes 4128772
  23.6 289.9 %reduce-scatter.2.cloned.1.call-start = ((), (), s32[]{:S(2)}) async-start(), calls=%async_computation.4 | async-start | bytes 294912 | tf_op jit(solution)/shard_map/reduce_scatter | solution.py:64
  226.4 7.2 %copy-start.1 = (bf16[24,128,128]{2,1,0:T(8,128)(2,1)}, bf16[24,128,128]{2,1,0:T(8,128)(2,1)S(1)}, u32[]{:S(2)}) copy-start(bf16[24,128,128]{2,1,0:T(8,128)(2,1)S(1)} %convolution_convert_fusion.1) | copy-start | bytes 2359300
  240.4 5.9 %slice-start = ((bf16[42,128,128]{2,1,0:T(8,128)(2,1)}), bf16[12,128,128]{2,1,0:T(8,128)(2,1)S(1)}, s32[]{:S(2)}) async-start(bf16[42,128,128]{2,1,0:T(8,128)(2,1)} %param.13), calls=%async_computation.5 | async-start | bytes 786432 | tf_op jit(solution)/shard_map/slice | solution.py:26
  245.0 1.3 copy-start
  246.9 3.8 copy-start.5
  253.4 1.2 slice-start.1
  253.4 3.1 copy-start.9
  254.6 3.7 copy-start.3
  254.6 2.1 copy-start.6
  256.7 1.6 copy-start.7
  258.3 2.1 copy-start.4
  260.4 2.8 copy-start.12
  260.4 50.7 %copy-start.2 = (bf16[24,128,128]{2,1,0:T(8,128)(2,1)S(1)}, bf16[24,128,128]{2,1,0:T(8,128)(2,1)}, u32[]{:S(2)}) copy-start(bf16[24,128,128]{2,1,0:T(8,128)(2,1)} %copy-done.1) | copy-start | bytes 2359300
  262.4 51.1 %copy-start.10 = (bf16[1,128,128]{2,1,0:T(8,128)(2,1)S(1)}, bf16[1,128,128]{2,1,0:T(8,128)(2,1)}, u32[]{:S(2)}) copy-start(bf16[1,128,128]{2,1,0:T(8,128)(2,1)} %param.14) | copy-start | bytes 98308
Sparse Core Ops, SparseCore 0:
  11.2 81.4 all-gather.3
  95.3 74.3 all-gather.5
  263.3 32.9 reduce-scatter.1
